TPU v7x, 32 devices: a whole 2x2x4 slice. The times are simulated.
32 devices in a mesh: fz: 8 (over y, x, core), fxy: 4 (over z).
Axes of the slice: x: 2, y: 2, z: 4, core: 2. Of those that a mesh axis runs over, the one named last changes fastest.
Arguments:
- e_field: float32 [3, 64, 64, 512], P(None, 'fz', 'fxy'), may hold values from -6 to 6
- h_field: float32 [3, 64, 64, 512], P(None, 'fz', 'fxy'), may hold values from -6 to 6
- e_decay: float32 [64, 64, 512], P('fz', 'fxy'), may hold values from 0.6 to 1
- e_gain: float32 [64, 64, 512], P('fz', 'fxy'), may hold values from 0.2 to 0.6
- port_cell: int32 [8, 256], P('fz', 'fxy'), may hold values from 0 to 65535
- port_node: int32 [8, 256], P('fz', 'fxy'), may hold values from 0 to 2047
- port_conductance: float32 [8, 256], P('fz', 'fxy'), may hold values from 0.5 to 2
- inverse: float32 [8, 2048, 2048], P('fz', 'fxy'), may hold values from -1 to 2, as said below
- line_near: int32 [8, 128], P('fz'), may hold values from 0 to 2047
- line_far: int32 [8, 128], P('fz'), may hold values from 0 to 2047
- line_delay: int32 [8, 128], P('fz'), may hold values from 1 to 6
- line_imped: float32 [8, 128], P('fz'), may hold values from 0.5 to 4
- hist_near: float32 [8, 6, 128], P('fz'), may hold values from -6 to 6
- hist_far: float32 [8, 6, 128], P('fz'), may hold values from -6 to 6
Outputs:
- e_out: float32 [3, 64, 64, 512], P(None, 'fz', 'fxy')
- h_out: float32 [3, 64, 64, 512], P(None, 'fz', 'fxy')
- node_volt: float32 [8, 2048], P('fz', 'fxy')
- line_wave: float32 [8, 2, 128], P('fz')
Inputs may be any that keep to these rules, and one draw needn't show every extreme that they name: inverse[s] is symmetric for every s.
All inputs are finite; a program needn't handle non-finite values.
Results may differ from a plain program's by a relative error of at most 0.00029.
Values sent between devices are 32-bit elements; how exact they have to be, the bound alone decides.
A program may use at most 64 MiB of HBM per device.

v0:
```python
import functools

import jax
import jax.numpy as jnp
from jax import lax
from jax.experimental import pallas as pl
from jax.experimental.pallas import tpu as pltpu
from jax.sharding import PartitionSpec as P

STEPS = 4
LANES = 128
F32 = jnp.float32
BF16 = jnp.bfloat16
MESH = pl.DeviceIdType.MESH


def split3(x):
    a = x.astype(BF16)
    r = x - a.astype(F32)
    b = r.astype(BF16)
    c = (r - b.astype(F32)).astype(BF16)
    return a, b, c


def dot3(x, onehot, transposed):
    rows = x.shape[0]
    dims = (((1,), (1 if transposed else 0,)), ((), ()))
    if rows % 16 == 0:
        y = lax.dot_general(
            jnp.concatenate(split3(x), 0), onehot, dims, preferred_element_type=F32
        )
        return y[:rows] + y[rows : 2 * rows] + y[2 * rows :]
    a, b, c = (
        lax.dot_general(t, onehot, dims, preferred_element_type=F32) for t in split3(x)
    )
    return a + b + c


def kernel(
    e_in, h_in, decay_in, gain_in, port_cell, port_node, port_cond, inv_in,
    line_near, line_far, line_delay, line_imped, hist_near, hist_far,
    e_out, h_out, volt_out, wave_out,
    e, h, decay, gain, inv, cell_row, cell_y, node_hi, node_lo, pads,
    hx_send, hx, ex_send, ex, part_send, part, far_send, far, volt_send, volt,
    up_send, above, acc,
    load_sem, out_sem, face_send, face_recv, part_ss, part_rs, volt_ss, volt_rs,
):
    s, j = lax.axis_index("fz"), lax.axis_index("fxy")
    ns, nj = lax.axis_size("fz"), lax.axis_size("fxy")
    above_id, below_id = lax.rem(s + 1, ns), lax.rem(s + ns - 1, ns)
    right_id, left_id = lax.rem(j + 1, nj), lax.rem(j + nj - 1, nj)
    _, cz, cx, ny = e_in.shape
    cells = cz * cx
    block, nodes = inv_in.shape[1:]
    ports = port_cell.shape[1]
    lines = line_near.shape[1]
    depth = hist_near.shape[1]

    loads = [
        pltpu.make_async_copy(e_in, e.at[:, 0:cz], load_sem.at[0]),
        pltpu.make_async_copy(h_in, h.at[:, 1 : cz + 1], load_sem.at[1]),
        pltpu.make_async_copy(gain_in, gain, load_sem.at[2]),
        pltpu.make_async_copy(inv_in.at[0], inv, load_sem.at[3]),
        pltpu.make_async_copy(decay_in, decay, load_sem.at[4]),
    ]
    for copy in loads:
        copy.start()

    h[:, 0] = jnp.zeros((3, cx, ny), F32)
    e[:, cz] = jnp.zeros((3, cx, ny), F32)
    hx[...] = jnp.zeros(hx.shape, F32)
    ex[...] = jnp.zeros(ex.shape, F32)
    far[...] = jnp.zeros(far.shape, F32)
    above[...] = jnp.zeros(above.shape, F32)

    barrier = pltpu.get_barrier_semaphore()
    for other in (above_id, below_id):
        pl.semaphore_signal(barrier, inc=1, device_id={"fz": other}, device_id_type=MESH)
    for d in range(1, nj):
        pl.semaphore_signal(
            barrier, inc=1, device_id={"fxy": lax.rem(j + d, nj)}, device_id_type=MESH
        )

    pads[...] = jnp.full(pads.shape, -1, jnp.int32)
    pads[0:1, 0:ports] = port_cell[...]
    pads[1:2, 0:ports] = port_node[...]
    cell = pads[0:1, :]
    pnode = pads[1:2, :]
    valid = cell >= 0
    row = jnp.where(valid, cell // ny, -1)
    col = jnp.where(valid, cell % ny, -1)
    cell_row[...] = (lax.broadcasted_iota(jnp.int32, (cells, LANES), 0) == row).astype(F32)
    cell_y[...] = (
        (lax.broadcasted_iota(jnp.int32, (ny, LANES), 0) == col).astype(F32).astype(BF16)
    )
    for k, index in enumerate((pnode, line_near[...], line_far[...])):
        hi = jnp.where(index >= 0, index // block, -1)
        lo = jnp.where(index >= 0, index % block, -1)
        at = pl.ds(k * LANES, LANES)
        node_hi[:, at] = (
            lax.broadcasted_iota(jnp.int32, (node_hi.shape[0], LANES), 0) == hi
        ).astype(F32)
        node_lo[:, at] = (
            (lax.broadcasted_iota(jnp.int32, (block, LANES), 0) == lo)
            .astype(F32)
            .astype(BF16)
        )
    part_send[...] = jnp.zeros(part_send.shape, F32)
    part_send[0, 0:1, 0:ports] = port_cond[...]
    cond = part_send[0, 0:1, 0:LANES]

    has_above, has_below = s < ns - 1, s > 0
    has_right, has_left = j < nj - 1, j > 0

    def face(kind, step, src, dst, axis, other):
        return pltpu.make_async_remote_copy(
            src_ref=src, dst_ref=dst,
            send_sem=face_send.at[kind, step], recv_sem=face_recv.at[kind, step],
            device_id={axis: other}, device_id_type=MESH,
        )

    def up_copies(n):
        return (
            face(0, n, h.at[0:2, cz], h.at[0:2, 0], "fz", above_id),
            face(1, n, hx_send.at[n], hx.at[n], "fxy", right_id),
        )

    def down_copies(n):
        return (
            face(2, n, e.at[0:2, 0], e.at[0:2, cz], "fz", below_id),
            face(3, n, ex_send.at[n], ex.at[n], "fxy", left_id),
        )

    def far_copy(n):
        return face(4, n, far_send.at[n], far.at[n], "fz", above_id)

    def above_copy(n):
        return face(5, n, up_send.at[n], above.at[n], "fz", below_id)

    def start(cond_, copy):
        @pl.when(cond_)
        def _():
            copy.start()

    def wait_recv(cond_, copy):
        @pl.when(cond_)
        def _():
            copy.wait_recv()

    def wait_send(cond_, copy):
        @pl.when(cond_)
        def _():
            copy.wait_send()

    def gather_cells(plane):
        y = dot3(plane.reshape(cells, ny), cell_y[...], False)
        return jnp.sum(y * cell_row[...], axis=0, keepdims=True)

    def gather_nodes(volts, at):
        y = dot3(volts, node_lo[:, at], False)
        return jnp.sum(y * node_hi[0:nj, at], axis=0, keepdims=True)

    def scatter_nodes(values, at):
        rows = node_hi[:, at] * values
        return dot3(rows, node_lo[:, at], True)[0:nj]

    def gathers(n, send, recv, ss, rs):
        return [
            pltpu.make_async_remote_copy(
                src_ref=send.at[n], dst_ref=recv.at[n, j],
                send_sem=ss.at[n, d - 1], recv_sem=rs.at[n, d - 1],
                device_id={"fxy": lax.rem(j + d, nj)}, device_id_type=MESH,
            )
            for d in range(1, nj)
        ]

    at_port = pl.ds(0, LANES)
    at_near = pl.ds(LANES, LANES)
    at_far = pl.ds(2 * LANES, LANES)
    delay = line_delay[...]
    waves_a, waves_b = [], []

    def incoming(n, waves, hist):
        total = jnp.zeros((1, lines), F32)
        for k in range(1, depth + 1):
            value = waves[n - k] if n >= k else hist[0, k - n - 1 : k - n, :]
            total = jnp.where(delay == k, value, total)
        return total

    def send_far(n, in_b):
        far_send[n] = scatter_nodes(-in_b, at_far)
        start(has_above, far_copy(n))

    def send_ports(n):
        ez = gather_cells(e[2, 0:cz])
        own = scatter_nodes(cond * ez, at_port)
        part_send[n] = own
        for copy in gathers(n, part_send, part, part_ss, part_rs):
            copy.start()
        return ez, own

    lane = lax.broadcasted_iota(jnp.int32, (cx, ny), 1)
    sub = lax.broadcasted_iota(jnp.int32, (cx, ny), 0)

    in_b = incoming(0, waves_a, hist_near)
    in_a = incoming(0, waves_b, hist_far)
    pl.semaphore_wait(barrier, nj + 1)
    send_far(0, in_b)
    loads[0].wait()
    ez, own = send_ports(0)
    loads[1].wait()
    for c in range(2):
        for z in range(cz):
            hx_send[0, c, z : z + 1, :] = h[1 + c, z + 1, cx - 1 : cx, :]
    copy_z, copy_x = up_copies(0)
    start(has_above, copy_z)
    start(has_right, copy_x)
    loads[2].wait()
    gain_port = gather_cells(gain[...])
    loads[3].wait()
    loads[4].wait()

    for n in range(STEPS):
        near_src = scatter_nodes(-in_a, at_near)
        wait_recv(has_below, far_copy(n))
        port_copies = gathers(n, part_send, part, part_ss, part_rs)
        for copy in port_copies:
            copy.wait_recv()
        part[n, j] = own
        totals = part[n, 0]
        for k in range(1, nj):
            totals = totals + part[n, k]
        totals = totals + (near_src + far[n])
        chunk = 32

        @pl.loop(0, block // chunk)
        def _(r):
            at = pl.ds(pl.multiple_of(r * chunk, chunk), chunk)
            value = jnp.zeros((chunk, LANES), F32)
            for k in range(nodes // LANES):
                q, w = divmod(k * LANES, block)
                value = value + inv[at, k * LANES : (k + 1) * LANES] * totals[
                    q : q + 1, w : w + LANES
                ]
            acc[at, :] = value

        terms = jnp.concatenate(split3(acc[...]), 1)
        local_volt = lax.dot_general(
            jnp.ones((16, 3 * LANES), BF16), terms, (((1,), (1,)), ((), ())),
            preferred_element_type=F32,
        )[0:1]
        volt_send[n] = local_volt
        volt_copies = gathers(n, volt_send, volt, volt_ss, volt_rs)
        for copy in volt_copies:
            copy.start()

        copy_z, copy_x = up_copies(n)
        wait_recv(has_below, copy_z)
        wait_recv(has_left, copy_x)

        @pl.loop(0, cz)
        def _(z):
            hx_, hy_, hz_ = (h[c, z + 1] for c in range(3))
            lx, ly = h[0, z], h[1, z]
            fy = hx[n, 0, pl.ds(z, 1), :]
            fz = hx[n, 1, pl.ds(z, 1), :]

            def by(f):
                return f - jnp.where(lane == 0, 0.0, pltpu.roll(f, 1, 1))

            def bx(f, side):
                return f - jnp.where(sub == 0, side, pltpu.roll(f, 1, 0))

            g, q = gain[z], decay[z]
            e[0, z] = q * e[0, z] + g * (by(hz_) - (hy_ - ly))
            e[1, z] = q * e[1, z] + g * ((hx_ - lx) - bx(hz_, fz))
            e[2, z] = q * e[2, z] + g * (bx(hy_, fy) - by(hx_))

        for copy in volt_copies:
            copy.wait_recv()
        volt[n, j] = local_volt
        volts = jnp.concatenate([volt[n, k] for k in range(nj)], 0)
        up_send[n] = volts
        start(has_below, above_copy(n))
        drop = gain_port * (cond * (ez - gather_nodes(volts, at_port)))
        change = dot3(cell_row[...] * drop, cell_y[...], True)
        e[2, 0:cz] = e[2, 0:cz] - change.reshape(cz, cx, ny)
        for c in range(2):
            for z in range(cz):
                ex_send[n, c, z : z + 1, :] = e[1 + c, z, 0:1, :]
        down_z, down_x = down_copies(n)
        start(has_below, down_z)
        start(has_left, down_x)

        out_a = -2.0 * gather_nodes(volts, at_near) / line_imped[...] - in_a
        waves_a.append(out_a)
        old_b, old_ez = in_b, ez
        if n + 1 < STEPS:
            ez, own = send_ports(n + 1)
            in_b = incoming(n + 1, waves_a, hist_near)
            send_far(n + 1, in_b)
        else:
            e_store = pltpu.make_async_copy(e.at[:, 0:cz], e_out, out_sem.at[0])
            e_store.start()

        wait_send(has_above, copy_z)
        wait_send(has_right, copy_x)
        wait_recv(has_above, down_z)
        wait_recv(has_right, down_x)

        @pl.loop(0, cz)
        def _(z):
            ex_, ey_, ez_ = (e[c, z] for c in range(3))
            ux, uy = e[0, z + 1], e[1, z + 1]
            fy = ex[n, 0, pl.ds(z, 1), :]
            fz = ex[n, 1, pl.ds(z, 1), :]

            def dy(f):
                return jnp.where(lane == ny - 1, 0.0, pltpu.roll(f, ny - 1, 1)) - f

            def dx(f, side):
                return jnp.where(sub == cx - 1, side, pltpu.roll(f, cx - 1, 0)) - f

            h[0, z + 1] = h[0, z + 1] - 0.5 * (dy(ez_) - (uy - ey_))
            new_y = h[1, z + 1] - 0.5 * ((ux - ex_) - dx(ez_, fz))
            new_z = h[2, z + 1] - 0.5 * (dx(ey_, fy) - dy(ex_))
            h[1, z + 1] = new_y
            h[2, z + 1] = new_z
            if n + 1 < STEPS:
                hx_send[n + 1, 0, pl.ds(z, 1), :] = new_y[cx - 1 : cx, :]
                hx_send[n + 1, 1, pl.ds(z, 1), :] = new_z[cx - 1 : cx, :]

        if n + 1 < STEPS:
            next_z, next_x = up_copies(n + 1)
            start(has_above, next_z)
            start(has_right, next_x)
        else:
            h_store = pltpu.make_async_copy(h.at[:, 1 : cz + 1], h_out, out_sem.at[1])
            h_store.start()

        wait_recv(has_above, above_copy(n))
        out_b = -2.0 * gather_nodes(above[n], at_far) / line_imped[...] - old_b
        waves_b.append(out_b)
        if n + 1 < STEPS:
            in_a = incoming(n + 1, waves_b, hist_far)

        wait_send(has_below, down_z)
        wait_send(has_left, down_x)
        wait_send(has_above, far_copy(n))
        wait_send(has_below, above_copy(n))
        for copy in port_copies + volt_copies:
            copy.wait_send()

    volt_out[...] = local_volt
    wave_out[0, 0:1, :] = out_a
    wave_out[0, 1:2, :] = out_b
    e_store.wait()
    h_store.wait()


def local(*args):
    e_field, inverse = args[0], args[7]
    nj = lax.axis_size("fxy")
    _, cz, cx, ny = e_field.shape
    _, block, nodes = inverse.shape
    lines = args[8].shape[1]
    vmem, any_ = pl.BlockSpec(memory_space=pltpu.VMEM), pl.BlockSpec(memory_space=pl.ANY)
    in_any = (0, 1, 2, 3, 7)
    rows = -(-nj // 16) * 16
    dma = pltpu.SemaphoreType.DMA
    v = pltpu.VMEM
    return pl.pallas_call(
        kernel,
        out_shape=(
            jax.ShapeDtypeStruct(e_field.shape, F32),
            jax.ShapeDtypeStruct(e_field.shape, F32),
            jax.ShapeDtypeStruct((1, block), F32),
            jax.ShapeDtypeStruct((1, 2, lines), F32),
        ),
        in_specs=[any_ if i in in_any else vmem for i in range(len(args))],
        out_specs=(any_, any_, vmem, vmem),
        scratch_shapes=[
            v((3, cz + 1, cx, ny), F32),
            v((3, cz + 1, cx, ny), F32),
            v((cz, cx, ny), F32),
            v((cz, cx, ny), F32),
            v((block, nodes), F32),
            v((cz * cx, LANES), F32),
            v((ny, LANES), BF16),
            v((rows, 3 * LANES), F32),
            v((block, 3 * LANES), BF16),
            v((8, LANES), jnp.int32),
            v((STEPS, 2, cz, ny), F32),
            v((STEPS, 2, cz, ny), F32),
            v((STEPS, 2, cz, ny), F32),
            v((STEPS, 2, cz, ny), F32),
            v((STEPS, nj, block), F32),
            v((STEPS, nj, nj, block), F32),
            v((STEPS, nj, block), F32),
            v((STEPS, nj, block), F32),
            v((STEPS, 1, block), F32),
            v((STEPS, nj, 1, block), F32),
            v((STEPS, nj, block), F32),
            v((STEPS, nj, block), F32),
            v((block, LANES), F32),
            dma((5,)),
            dma((2,)),
            dma((6, STEPS)),
            dma((6, STEPS)),
            dma((STEPS, nj - 1)),
            dma((STEPS, nj - 1)),
            dma((STEPS, nj - 1)),
            dma((STEPS, nj - 1)),
        ],
        compiler_params=pltpu.CompilerParams(
            collective_id=0, has_side_effects=True, vmem_limit_bytes=48 * 1024 * 1024
        ),
    )(*args)


def solution(mesh):
    placed = (
        P(None, "fz", "fxy", None),
        P(None, "fz", "fxy", None),
        P("fz", "fxy", None),
        P("fz", "fxy", None),
        P("fz", "fxy"),
        P("fz", "fxy"),
        P("fz", "fxy"),
        P("fz", "fxy", None),
        P("fz", None),
        P("fz", None),
        P("fz", None),
        P("fz", None),
        P("fz", None, None),
        P("fz", None, None),
    )
    return jax.shard_map(
        local,
        mesh=mesh,
        in_specs=placed,
        out_specs=(
            P(None, "fz", "fxy", None),
            P(None, "fz", "fxy", None),
            P("fz", "fxy"),
            P("fz", None, None),
        ),
        check_vma=False,
    )
```

profile of v0, /device:TPU:0, one launch (start us, length us, event | category | flops | bytes accessed | tf_op | source)
XLA Modules:
  0.0 59.4 jit_solution(5422457885278493712)
XLA Ops:
  0.6 0.7 %copy.18.hist_near = f32[1,6,128]{2,1,0:T(8,128)S(1)} copy(f32[1,6,128]{2,0,1:T(1,128)} %param.26) | data formatting | bytes 6144 | tf_op args[12]
  1.3 0.7 %copy.19.hist_far = f32[1,6,128]{2,1,0:T(8,128)S(1)} copy(f32[1,6,128]{2,0,1:T(1,128)} %param.27) | data formatting | bytes 6144 | tf_op args[13]
  2.0 0.0 copy-start
  2.0 1.1 %copy-done = f32[3,8,16,512]{3,2,1,0:T(8,128)S(1)} copy-done((f32[3,8,16,512]{3,2,1,0:T(8,128)S(1)}, f32[3,8,16,512]{3,2,1,0:T(8,128)}, u32[]{:S(2)}) %copy-start) | copy-done | bytes 786456
  3.1 0.0 copy-start.1
  3.1 1.1 %copy-done.1 = f32[3,8,16,512]{3,2,1,0:T(8,128)S(1)} copy-done((f32[3,8,16,512]{3,2,1,0:T(8,128)S(1)}, f32[3,8,16,512]{3,2,1,0:T(8,128)}, u32[]{:S(2)}) %copy-start.1) | copy-done | bytes 786456
  4.3 0.0 copy-start.2
  4.3 0.9 %copy-done.2 = f32[8,16,512]{2,1,0:T(8,128)S(1)} copy-done((f32[8,16,512]{2,1,0:T(8,128)S(1)}, f32[8,16,512]{2,1,0:T(8,128)}, u32[]{:S(2)}) %copy-start.2) | copy-done | bytes 262168
  5.2 0.0 copy-start.3
  5.2 0.9 %copy-done.3 = f32[8,16,512]{2,1,0:T(8,128)S(1)} copy-done((f32[8,16,512]{2,1,0:T(8,128)S(1)}, f32[8,16,512]{2,1,0:T(8,128)}, u32[]{:S(2)}) %copy-start.3) | copy-done | bytes 262168
  6.2 0.0 copy-start.4
  6.2 0.7 %copy-done.4 = s32[1,64]{1,0:T(1,128)S(1)} copy-done((s32[1,64]{1,0:T(1,128)S(1)}, s32[1,64]{1,0:T(1,128)}, u32[]{:S(2)}) %copy-start.4) | copy-done | bytes 280
  6.8 0.0 copy-start.5
  6.8 0.7 %copy-done.5 = s32[1,64]{1,0:T(1,128)S(1)} copy-done((s32[1,64]{1,0:T(1,128)S(1)}, s32[1,64]{1,0:T(1,128)}, u32[]{:S(2)}) %copy-start.5) | copy-done | bytes 280
  7.5 0.7 %copy-done.6 = f32[1,64]{1,0:T(1,128)S(1)} copy-done((f32[1,64]{1,0:T(1,128)S(1)}, f32[1,64]{1,0:T(1,128)}, u32[]{:S(2)}) %copy-start.6) | copy-done | bytes 280
  8.1 0.7 %copy-done.7 = s32[1,128]{1,0:T(1,128)S(1)} copy-done((s32[1,128]{1,0:T(1,128)S(1)}, s32[1,128]{1,0:T(1,128)}, u32[]{:S(2)}) %copy-start.7) | copy-done | bytes 536
  8.8 0.7 %copy-done.8 = s32[1,128]{1,0:T(1,128)S(1)} copy-done((s32[1,128]{1,0:T(1,128)S(1)}, s32[1,128]{1,0:T(1,128)}, u32[]{:S(2)}) %copy-start.8) | copy-done | bytes 536
  9.5 0.7 %copy-done.9 = s32[1,128]{1,0:T(1,128)S(1)} copy-done((s32[1,128]{1,0:T(1,128)S(1)}, s32[1,128]{1,0:T(1,128)}, u32[]{:S(2)}) %copy-start.9) | copy-done | bytes 536
  10.1 0.7 %copy-done.10 = f32[1,128]{1,0:T(1,128)S(1)} copy-done((f32[1,128]{1,0:T(1,128)S(1)}, f32[1,128]{1,0:T(1,128)}, u32[]{:S(2)}) %copy-start.10) | copy-done | bytes 536
  10.8 45.7 %shard_map.165 = (f32[3,8,16,512]{3,2,1,0:T(8,128)S(1)}, f32[3,8,16,512]{3,2,1,0:T(8,128)S(1)}, f32[1,512]{1,0:T(1,128)S(1)}, f32[1,2,128]{2,1,0:T(2,128)S(1)}) custom-call(f32[3,8,16,512]{3,2,1,0:T(8,128)S(1)} %copy-done, f32[3,8,16,512]{3,2,1,0:T(8,128)S(1)} %copy-done.1, f32[8,16,512]{2,1,0:T(8,128)S(1)} %copy-done.2, f32[8,16,512]{2,1,0:T(8,128)S(1)} %copy-done.3, ...), custom_call_target="tpu_custom_call" | custom-call | tf_op jit(solution)/shard_map/pallas_call | solution.py:372
  56.5 0.9 %copy.24 = f32[3,8,16,512]{3,2,1,0:T(8,128)} copy(f32[3,8,16,512]{3,2,1,0:T(8,128)S(1)} %get-tuple-element.8) | data formatting | bytes 1572864
  57.4 0.9 %copy.25 = f32[3,8,16,512]{3,2,1,0:T(8,128)} copy(f32[3,8,16,512]{3,2,1,0:T(8,128)S(1)} %get-tuple-element.9) | data formatting | bytes 1572864
  58.3 0.6 copy.26
  58.8 0.6 copy.27
  (5 shorter events, 0.0 us)
Async XLA Ops:
  2.0 1.1 %copy-start = (f32[3,8,16,512]{3,2,1,0:T(8,128)S(1)}, f32[3,8,16,512]{3,2,1,0:T(8,128)}, u32[]{:S(2)}) copy-start(f32[3,8,16,512]{3,2,1,0:T(8,128)} %e_in.1) | copy-start | bytes 2359300
  3.1 1.1 %copy-start.1 = (f32[3,8,16,512]{3,2,1,0:T(8,128)S(1)}, f32[3,8,16,512]{3,2,1,0:T(8,128)}, u32[]{:S(2)}) copy-start(f32[3,8,16,512]{3,2,1,0:T(8,128)} %h_in.1) | copy-start | bytes 2359300
  4.3 0.9 %copy-start.2 = (f32[8,16,512]{2,1,0:T(8,128)S(1)}, f32[8,16,512]{2,1,0:T(8,128)}, u32[]{:S(2)}) copy-start(f32[8,16,512]{2,1,0:T(8,128)} %decay_in.1) | copy-start | bytes 786436
  5.2 0.9 %copy-start.3 = (f32[8,16,512]{2,1,0:T(8,128)S(1)}, f32[8,16,512]{2,1,0:T(8,128)}, u32[]{:S(2)}) copy-start(f32[8,16,512]{2,1,0:T(8,128)} %gain_in.1) | copy-start | bytes 786436
  6.2 0.7 %copy-start.4 = (s32[1,64]{1,0:T(1,128)S(1)}, s32[1,64]{1,0:T(1,128)}, u32[]{:S(2)}) copy-start(s32[1,64]{1,0:T(1,128)} %port_cell.1) | copy-start | bytes 772
  6.8 0.7 %copy-start.5 = (s32[1,64]{1,0:T(1,128)S(1)}, s32[1,64]{1,0:T(1,128)}, u32[]{:S(2)}) copy-start(s32[1,64]{1,0:T(1,128)} %port_node.1) | copy-start | bytes 772
  7.5 0.7 %copy-start.6 = (f32[1,64]{1,0:T(1,128)S(1)}, f32[1,64]{1,0:T(1,128)}, u32[]{:S(2)}) copy-start(f32[1,64]{1,0:T(1,128)} %port_cond.1) | copy-start | bytes 772
  8.1 0.7 %copy-start.7 = (s32[1,128]{1,0:T(1,128)S(1)}, s32[1,128]{1,0:T(1,128)}, u32[]{:S(2)}) copy-start(s32[1,128]{1,0:T(1,128)} %line_near.1) | copy-start | bytes 1540
  8.8 0.7 %copy-start.8 = (s32[1,128]{1,0:T(1,128)S(1)}, s32[1,128]{1,0:T(1,128)}, u32[]{:S(2)}) copy-start(s32[1,128]{1,0:T(1,128)} %line_far.1) | copy-start | bytes 1540
  9.4 0.7 %copy-start.9 = (s32[1,128]{1,0:T(1,128)S(1)}, s32[1,128]{1,0:T(1,128)}, u32[]{:S(2)}) copy-start(s32[1,128]{1,0:T(1,128)} %line_delay.1) | copy-start | bytes 1540
  10.1 0.7 %copy-start.10 = (f32[1,128]{1,0:T(1,128)S(1)}, f32[1,128]{1,0:T(1,128)}, u32[]{:S(2)}) copy-start(f32[1,128]{1,0:T(1,128)} %line_imped.1) | copy-start | bytes 1540
where the time goes:
time: 60.4 us; the launch traced here: 59.4 us
  Pallas kernels  45.7 us (76%)
  local copies, waits for them, and re-layouts  13 us (22%)
  between operations  0.65 us (1%)
    pallas_call x1, Pallas kernels, local(): pl.pallas_call(kernel, out_shape=(jax.ShapeDtypeStruct(e_field.shape, F32...  45.7 us
    unnamed x28, local copies, waits for them, and re-layouts  13 us

commit v1 on v0

--- a/solution.py
+++ b/solution.py
@@ -37,10 +37,12 @@
 
 
 def kernel(
-    e_in, h_in, decay_in, gain_in, port_cell, port_node, port_cond, inv_in,
-    line_near, line_far, line_delay, line_imped, hist_near, hist_far,
+    e_in, h_in, decay_in, gain_in, port_cell_in, port_node_in, port_cond_in, inv_in,
+    line_near_in, line_far_in, line_delay_in, line_imped_in, hist_near_in, hist_far_in,
     e_out, h_out, volt_out, wave_out,
-    e, h, decay, gain, inv, cell_row, cell_y, node_hi, node_lo, pads,
+    port_cell, port_node, port_cond, line_near, line_far, line_delay, line_imped,
+    hist_near, hist_far,
+    e, h, hz, ez_up, decay, gain, inv, cell_row, cell_y, node_hi, node_lo, pads,
     hx_send, hx, ex_send, ex, part_send, part, far_send, far, volt_send, volt,
     up_send, above, acc,
     load_sem, out_sem, face_send, face_recv, part_ss, part_rs, volt_ss, volt_rs,
@@ -52,9 +54,9 @@
     _, cz, cx, ny = e_in.shape
     cells = cz * cx
     block, nodes = inv_in.shape[1:]
-    ports = port_cell.shape[1]
-    lines = line_near.shape[1]
-    depth = hist_near.shape[1]
+    ports = port_cell_in.shape[1]
+    lines = line_near_in.shape[1]
+    depth = hist_near_in.shape[0]
 
     loads = [
         pltpu.make_async_copy(e_in, e.at[:, 0:cz], load_sem.at[0]),
@@ -63,13 +65,20 @@
         pltpu.make_async_copy(inv_in.at[0], inv, load_sem.at[3]),
         pltpu.make_async_copy(decay_in, decay, load_sem.at[4]),
     ]
-    for copy in loads:
+    small = (
+        (port_cell_in, port_cell), (port_node_in, port_node), (port_cond_in, port_cond),
+        (line_near_in, line_near), (line_far_in, line_far), (line_delay_in, line_delay),
+        (line_imped_in, line_imped), (hist_near_in, hist_near), (hist_far_in, hist_far),
+    )
+    small = [
+        pltpu.make_async_copy(src, dst, load_sem.at[5 + k])
+        for k, (src, dst) in enumerate(small)
+    ]
+    for copy in small + loads:
         copy.start()
 
     h[:, 0] = jnp.zeros((3, cx, ny), F32)
     e[:, cz] = jnp.zeros((3, cx, ny), F32)
-    hx[...] = jnp.zeros(hx.shape, F32)
-    ex[...] = jnp.zeros(ex.shape, F32)
     far[...] = jnp.zeros(far.shape, F32)
     above[...] = jnp.zeros(above.shape, F32)
 
@@ -80,6 +89,9 @@
         pl.semaphore_signal(
             barrier, inc=1, device_id={"fxy": lax.rem(j + d, nj)}, device_id_type=MESH
         )
+
+    for copy in small:
+        copy.wait()
 
     pads[...] = jnp.full(pads.shape, -1, jnp.int32)
     pads[0:1, 0:ports] = port_cell[...]
@@ -121,13 +133,13 @@
 
     def up_copies(n):
         return (
-            face(0, n, h.at[0:2, cz], h.at[0:2, 0], "fz", above_id),
+            face(0, n, h.at[0:2, cz], hz.at[n], "fz", above_id),
             face(1, n, hx_send.at[n], hx.at[n], "fxy", right_id),
         )
 
     def down_copies(n):
         return (
-            face(2, n, e.at[0:2, 0], e.at[0:2, cz], "fz", below_id),
+            face(2, n, e.at[0:2, 0], ez_up.at[n], "fz", below_id),
             face(3, n, ex_send.at[n], ex.at[n], "fxy", left_id),
         )
 
@@ -183,7 +195,7 @@
     def incoming(n, waves, hist):
         total = jnp.zeros((1, lines), F32)
         for k in range(1, depth + 1):
-            value = waves[n - k] if n >= k else hist[0, k - n - 1 : k - n, :]
+            value = waves[n - k] if n >= k else hist[k - n - 1]
             total = jnp.where(delay == k, value, total)
         return total
 
@@ -255,26 +267,40 @@
             copy.start()
 
         copy_z, copy_x = up_copies(n)
-        wait_recv(has_below, copy_z)
-        wait_recv(has_left, copy_x)
 
         @pl.loop(0, cz)
         def _(z):
             hx_, hy_, hz_ = (h[c, z + 1] for c in range(3))
             lx, ly = h[0, z], h[1, z]
-            fy = hx[n, 0, pl.ds(z, 1), :]
-            fz = hx[n, 1, pl.ds(z, 1), :]
 
             def by(f):
                 return f - jnp.where(lane == 0, 0.0, pltpu.roll(f, 1, 1))
 
-            def bx(f, side):
-                return f - jnp.where(sub == 0, side, pltpu.roll(f, 1, 0))
+            def bx(f):
+                return f - jnp.where(sub == 0, 0.0, pltpu.roll(f, 1, 0))
 
             g, q = gain[z], decay[z]
             e[0, z] = q * e[0, z] + g * (by(hz_) - (hy_ - ly))
-            e[1, z] = q * e[1, z] + g * ((hx_ - lx) - bx(hz_, fz))
-            e[2, z] = q * e[2, z] + g * (bx(hy_, fy) - by(hx_))
+            e[1, z] = q * e[1, z] + g * ((hx_ - lx) - bx(hz_))
+            e[2, z] = q * e[2, z] + g * (bx(hy_) - by(hx_))
+
+        down_z, down_x = down_copies(n)
+
+        @pl.when(has_left)
+        def _():
+            copy_x.wait_recv()
+            for z in range(cz):
+                g = gain[z, 0:1, :]
+                e[1, z, 0:1, :] = e[1, z, 0:1, :] + g * hx[n, 1, z : z + 1, :]
+                e[2, z, 0:1, :] = e[2, z, 0:1, :] - g * hx[n, 0, z : z + 1, :]
+
+        @pl.when(has_below)
+        def _():
+            copy_z.wait_recv()
+            g = gain[0]
+            e[0, 0] = e[0, 0] + g * hz[n, 1]
+            e[1, 0] = e[1, 0] - g * hz[n, 0]
+            down_z.start()
 
         for copy in volt_copies:
             copy.wait_recv()
@@ -288,8 +314,6 @@
         for c in range(2):
             for z in range(cz):
                 ex_send[n, c, z : z + 1, :] = e[1 + c, z, 0:1, :]
-        down_z, down_x = down_copies(n)
-        start(has_below, down_z)
         start(has_left, down_x)
 
         out_a = -2.0 * gather_nodes(volts, at_near) / line_imped[...] - in_a
@@ -305,35 +329,48 @@
 
         wait_send(has_above, copy_z)
         wait_send(has_right, copy_x)
-        wait_recv(has_above, down_z)
-        wait_recv(has_right, down_x)
 
         @pl.loop(0, cz)
         def _(z):
             ex_, ey_, ez_ = (e[c, z] for c in range(3))
             ux, uy = e[0, z + 1], e[1, z + 1]
-            fy = ex[n, 0, pl.ds(z, 1), :]
-            fz = ex[n, 1, pl.ds(z, 1), :]
 
             def dy(f):
                 return jnp.where(lane == ny - 1, 0.0, pltpu.roll(f, ny - 1, 1)) - f
 
-            def dx(f, side):
-                return jnp.where(sub == cx - 1, side, pltpu.roll(f, cx - 1, 0)) - f
+            def dx(f):
+                return jnp.where(sub == cx - 1, 0.0, pltpu.roll(f, cx - 1, 0)) - f
 
             h[0, z + 1] = h[0, z + 1] - 0.5 * (dy(ez_) - (uy - ey_))
-            new_y = h[1, z + 1] - 0.5 * ((ux - ex_) - dx(ez_, fz))
-            new_z = h[2, z + 1] - 0.5 * (dx(ey_, fy) - dy(ex_))
-            h[1, z + 1] = new_y
-            h[2, z + 1] = new_z
-            if n + 1 < STEPS:
-                hx_send[n + 1, 0, pl.ds(z, 1), :] = new_y[cx - 1 : cx, :]
-                hx_send[n + 1, 1, pl.ds(z, 1), :] = new_z[cx - 1 : cx, :]
+            h[1, z + 1] = h[1, z + 1] - 0.5 * ((ux - ex_) - dx(ez_))
+            h[2, z + 1] = h[2, z + 1] - 0.5 * (dx(ey_) - dy(ex_))
+
+        @pl.when(has_above)
+        def _():
+            down_z.wait_recv()
+            h[0, cz] = h[0, cz] + 0.5 * ez_up[n, 1]
+            h[1, cz] = h[1, cz] - 0.5 * ez_up[n, 0]
 
         if n + 1 < STEPS:
             next_z, next_x = up_copies(n + 1)
+        at_x = slice(cx - 1, cx)
+
+        @pl.when(has_right)
+        def _():
+            down_x.wait_recv()
+            for z in range(cz):
+                new_y = h[1, z + 1, at_x, :] + 0.5 * ex[n, 1, z : z + 1, :]
+                new_z = h[2, z + 1, at_x, :] - 0.5 * ex[n, 0, z : z + 1, :]
+                h[1, z + 1, at_x, :] = new_y
+                h[2, z + 1, at_x, :] = new_z
+                if n + 1 < STEPS:
+                    hx_send[n + 1, 0, z : z + 1, :] = new_y
+                    hx_send[n + 1, 1, z : z + 1, :] = new_z
+            if n + 1 < STEPS:
+                next_x.start()
+
+        if n + 1 < STEPS:
             start(has_above, next_z)
-            start(has_right, next_x)
         else:
             h_store = pltpu.make_async_copy(h.at[:, 1 : cz + 1], h_out, out_sem.at[1])
             h_store.start()
@@ -364,8 +401,10 @@
     _, cz, cx, ny = e_field.shape
     _, block, nodes = inverse.shape
     lines = args[8].shape[1]
+    args = [*args[:12], *(a.transpose(1, 0, 2) for a in args[12:])]
     vmem, any_ = pl.BlockSpec(memory_space=pltpu.VMEM), pl.BlockSpec(memory_space=pl.ANY)
-    in_any = (0, 1, 2, 3, 7)
+    small = [a for i, a in enumerate(args) if i not in (0, 1, 2, 3, 7)]
+    hbm = pl.BlockSpec(memory_space=pltpu.HBM)
     rows = -(-nj // 16) * 16
     dma = pltpu.SemaphoreType.DMA
     v = pltpu.VMEM
@@ -377,11 +416,14 @@
             jax.ShapeDtypeStruct((1, block), F32),
             jax.ShapeDtypeStruct((1, 2, lines), F32),
         ),
-        in_specs=[any_ if i in in_any else vmem for i in range(len(args))],
+        in_specs=[hbm] * len(args),
         out_specs=(any_, any_, vmem, vmem),
         scratch_shapes=[
+            *[v(a.shape, a.dtype) for a in small],
             v((3, cz + 1, cx, ny), F32),
             v((3, cz + 1, cx, ny), F32),
+            v((STEPS, 2, cx, ny), F32),
+            v((STEPS, 2, cx, ny), F32),
             v((cz, cx, ny), F32),
             v((cz, cx, ny), F32),
             v((block, nodes), F32),
@@ -403,7 +445,7 @@
             v((STEPS, nj, block), F32),
             v((STEPS, nj, block), F32),
             v((block, LANES), F32),
-            dma((5,)),
+            dma((5 + len(small),)),
             dma((2,)),
             dma((6, STEPS)),
             dma((6, STEPS)),
@@ -413,7 +455,7 @@
             dma((STEPS, nj - 1)),
         ],
         compiler_params=pltpu.CompilerParams(
-            collective_id=0, has_side_effects=True, vmem_limit_bytes=48 * 1024 * 1024
+            collective_id=0, has_side_effects=True, vmem_limit_bytes=67043328
         ),
     )(*args)
 

time: 60.4 us -> 53.4 us (0.88); the launches traced: 59.4 us -> 53.2 us
  local copies, waits for them, and re-layouts: 13 us -> 6.64 us
    unnamed x28 -> x4, local copies, waits for them, and re-layouts: 13 us -> 6.64 us
where the time goes in v1:
time: 53.4 us; the launch traced here: 53.2 us
  Pallas kernels  45.9 us (86%)
  local copies, waits for them, and re-layouts  6.64 us (12%)
  between operations  0.65 us (1%)
    pallas_call x1, Pallas kernels, local(): pl.pallas_call(kernel, out_shape=(jax.ShapeDtypeStruct(e_field.shape, F32...  45.9 us
    unnamed x4, local copies, waits for them, and re-layouts  6.64 us

profile of v1, /device:TPU:0, one launch (start us, length us, event | category | flops | bytes accessed | tf_op | source)
XLA Modules:
  0.0 53.2 jit_solution(15893633973977465958)
XLA Ops:
  0.6 45.9 %shard_map.165 = (f32[3,8,16,512]{3,2,1,0:T(8,128)}, f32[3,8,16,512]{3,2,1,0:T(8,128)}, f32[1,512]{1,0:T(1,128)}, f32[1,2,128]{2,1,0:T(2,128)}) custom-call(f32[3,8,16,512]{3,2,1,0:T(8,128)} %e_in.1, f32[3,8,16,512]{3,2,1,0:T(8,128)} %h_in.1, f32[8,16,512]{2,1,0:T(8,128)} %decay_in.1, f32[8,16,512]{2,1,0:T(8,128)} %gain_in.1, s32[1,64]{1,0:T(1,128)} %port_cell_in.1, ...), custom_call_target="tpu_custom_call" | custom-call | tf_op jit(solution)/shard_map/pallas_call | solution.py:411
  46.5 2.1 %copy.22 = f32[3,8,16,512]{3,2,1,0:T(8,128)} copy(f32[3,8,16,512]{3,2,1,0:T(8,128)} %get-tuple-element.8) | data formatting | bytes 1572864
  48.6 2.1 %copy.23 = f32[3,8,16,512]{3,2,1,0:T(8,128)} copy(f32[3,8,16,512]{3,2,1,0:T(8,128)} %get-tuple-element.9) | data formatting | bytes 1572864
  50.7 1.2 %copy.24 = f32[1,512]{1,0:T(1,128)} copy(f32[1,512]{1,0:T(1,128)} %get-tuple-element.10) | data formatting | bytes 4096
  52.0 1.2 %copy.25 = f32[1,2,128]{2,1,0:T(2,128)} copy(f32[1,2,128]{2,1,0:T(2,128)} %get-tuple-element.11) | data formatting | bytes 2048
